TPU v7x, 512 devices: a whole 4x8x8 slice. The times are simulated.
512 devices in a mesh: wide: 64 (over z, y), rows: 8 (over x, core).
Axes of the slice: x: 4, y: 8, z: 8, core: 2. Of those that a mesh axis runs over, the one named last changes fastest.
Arguments:
- slabs: bfloat16 [64, 8, 10, 32, 128], P('wide', 'rows'), may hold values from -6 to 6
- dest: int32 [64, 8, 10], P('wide', 'rows'), may hold values from 0 to 63, as said below
- pos: int32 [64, 8, 10], P('wide', 'rows'), may hold values from 0 to 9, as said below
- lengths: int32 [64], P('wide'), may hold values from 1 to 5
- cot: bfloat16 [64, 5, 16, 32, 128], P('wide', None, 'rows'), may hold values from -6 to 6
- w_first: bfloat16 [3456, 128], P('wide'), may hold values from -0.109375 to 0.109375
- w_second: bfloat16 [3456, 128], P('wide'), may hold values from -0.109375 to 0.109375
Outputs:
- block_out: bfloat16 [64, 5, 16, 32, 128], P('wide', None, 'rows')
- grad_input: bfloat16 [64, 5, 16, 32, 128], P('wide', None, 'rows')
- grad_w_first: float32 [3456, 128], P('wide')
- grad_w_second: float32 [3456, 128], P('wide')
Inputs may be any that keep to these rules, and one draw needn't show every extreme that they name: `dest`: within a band no loader sends more than one slab to any clip; every clip receives exactly 10 slabs in each band. `pos`: for every clip and band the 10 slabs it receives carry the places 0 to 9, each once.
All inputs are finite; a program needn't handle non-finite values.
Results may differ from a plain program's by a relative error of at most 0.018.
Values may be sent and summed in bfloat16 or wider, within the bound.
A program may use at most 64 MiB of HBM per device.

v0:
```python
import math
import jax
import jax.numpy as jnp
from jax import lax
from jax.sharding import PartitionSpec as P


def with_halo(block, sides, width):
    for axis, dim in sides:
        count = lax.axis_size(axis)
        forward = [(i, i + 1) for i in range(count - 1)]
        backward = [(target, source) for source, target in forward]
        low = lax.ppermute(
            lax.slice_in_dim(block, block.shape[dim] - width, None, axis=dim), axis, forward
        )
        high = lax.ppermute(lax.slice_in_dim(block, 0, width, axis=dim), axis, backward)
        block = jnp.concatenate([low, block, high], axis=dim)
    return block


def silu_slope(values):
    sig = jax.nn.sigmoid(values)
    return sig * (1.0 + values * (1.0 - sig))


def conv_forward(extended, kernel):
    padded = jnp.concatenate([extended[:1], extended[:1], extended], axis=0)
    result = lax.conv_general_dilated(
        padded[None],
        kernel,
        (1, 1, 1),
        ((0, 0), (0, 0), (1, 1)),
        dimension_numbers=("NDHWC", "DHWIO", "NDHWC"),
        preferred_element_type=jnp.float32,
    )
    return result[0]


def conv_weight_grad(extended, upstream):
    padded = jnp.concatenate([extended[:1], extended[:1], extended], axis=0)
    result = lax.conv_general_dilated(
        padded[None],
        upstream[None],
        (1, 1, 1),
        ((0, 0), (0, 0), (1, 1)),
        dimension_numbers=("CDHWN", "IDHWO", "NDHWC"),
        preferred_element_type=jnp.float32,
    )
    channels = extended.shape[-1]
    return jnp.transpose(result, (1, 2, 3, 0, 4)).reshape(27 * channels, upstream.shape[-1])


def conv_data_grad(upstream_ext, kernel):
    padded = jnp.pad(upstream_ext, ((2, 2), (0, 0), (0, 0), (0, 0)))
    flipped = kernel[::-1, ::-1, ::-1]
    result = lax.conv_general_dilated(
        padded[None],
        flipped,
        (1, 1, 1),
        ((0, 0), (0, 0), (1, 1)),
        dimension_numbers=("NDHWC", "DHWOI", "NDHWC"),
        preferred_element_type=jnp.float32,
    )[0]
    head = (result[0] + result[1] + result[2])[None]
    return jnp.concatenate([head, result[3:]], axis=0)


def body(slabs, dest, pos, lengths, cot, w_first, w_second):
    wide_size = lax.axis_size("wide")
    band_count = lax.axis_size("rows")
    slab_count = slabs.shape[2]
    columns = slabs.shape[3]
    channels = slabs.shape[4]
    frames = cot.shape[1]
    band_rows = cot.shape[2]
    capacity = -(-slab_count // wide_size)
    slot_count = wide_size * capacity
    targets = dest[0, 0]
    places = pos[0, 0]
    ranking = jnp.arange(slab_count, dtype=jnp.int32)
    earlier = (targets[None, :] == targets[:, None]) & (ranking[None, :] < ranking[:, None])
    slab_rank = jnp.sum(earlier.astype(jnp.int32), axis=1)
    slot_of = targets * capacity + slab_rank
    placing = slot_of[None, :] == jnp.arange(slot_count, dtype=jnp.int32)[:, None]
    flat_slabs = slabs[0, 0].reshape(slab_count, columns * channels)
    outgoing = jnp.dot(placing.astype(jnp.bfloat16), flat_slabs, preferred_element_type=jnp.float32)
    outgoing = outgoing.astype(jnp.bfloat16).reshape(wide_size, capacity, columns * channels)
    labels = jnp.sum(jnp.where(placing, places[None, :] + 1, 0), axis=1) - 1
    labels = labels.reshape(wide_size, capacity)
    arrived, arrived_places = (
        lax.all_to_all(outgoing, "wide", split_axis=0, concat_axis=0, tiled=True),
        lax.all_to_all(labels, "wide", split_axis=0, concat_axis=0, tiled=True),
    )
    settle = (
        arrived_places.reshape(slot_count)[None, :]
        == jnp.arange(slab_count, dtype=jnp.int32)[:, None]
    )
    tile = jnp.dot(
        settle.astype(jnp.bfloat16),
        arrived.reshape(slot_count, columns * channels),
        preferred_element_type=jnp.float32,
    )
    tile = tile.astype(jnp.bfloat16).reshape(frames, band_rows, columns, channels)
    full_first, full_second = (
        lax.all_gather(w_first, "wide", axis=0, tiled=True),
        lax.all_gather(w_second, "wide", axis=0, tiled=True),
    )
    kernel_first = full_first.reshape(3, 3, 3, channels, channels)
    kernel_second = full_second.reshape(3, 3, 3, channels, channels)
    tile_wide = tile.astype(jnp.float32)
    first = jax.nn.silu(tile_wide).astype(jnp.bfloat16)
    first_ext = with_halo(first, (("rows", 1),), 1)
    act = conv_forward(first_ext, kernel_first).astype(jnp.bfloat16)
    second = jax.nn.silu(act.astype(jnp.float32)).astype(jnp.bfloat16)
    second_ext = with_halo(second, (("rows", 1),), 1)
    block_out = (tile_wide + conv_forward(second_ext, kernel_second)).astype(jnp.bfloat16)
    live = (jnp.arange(frames, dtype=jnp.int32) < lengths[0])[:, None, None, None]
    out_grad = jnp.where(live, cot[0], jnp.zeros_like(cot[0]))
    out_grad_ext = with_halo(out_grad, (("rows", 1),), 1)
    weight_second = conv_weight_grad(second_ext, out_grad)
    hidden_grad = conv_data_grad(out_grad_ext, kernel_second)
    act_grad = (hidden_grad * silu_slope(act.astype(jnp.float32))).astype(jnp.bfloat16)
    act_grad_ext = with_halo(act_grad, (("rows", 1),), 1)
    weight_first = conv_weight_grad(first_ext, act_grad)
    first_grad = conv_data_grad(act_grad_ext, kernel_first)
    grad_input = (out_grad.astype(jnp.float32) + first_grad * silu_slope(tile_wide)).astype(
        jnp.bfloat16
    )
    scale = 1.0 / math.sqrt(frames * band_rows * columns * band_count * wide_size)
    weight_first = weight_first * scale
    weight_second = weight_second * scale
    total_first, total_second = (
        lax.psum(weight_first.astype(jnp.bfloat16), "rows").astype(jnp.float32),
        lax.psum(weight_second.astype(jnp.bfloat16), "rows").astype(jnp.float32),
    )
    share_first, share_second = (
        lax.psum_scatter(total_first, "wide", scatter_dimension=0, tiled=True),
        lax.psum_scatter(total_second, "wide", scatter_dimension=0, tiled=True),
    )
    return (block_out[None], grad_input[None], share_first, share_second)


def solution(mesh):
    return jax.shard_map(
        body,
        mesh=mesh,
        in_specs=(
            P("wide", "rows", None, None, None),
            P("wide", "rows", None),
            P("wide", "rows", None),
            P("wide"),
            P("wide", None, "rows", None, None),
            P("wide", None),
            P("wide", None),
        ),
        out_specs=(
            P("wide", None, "rows", None, None),
            P("wide", None, "rows", None, None),
            P("wide", None),
            P("wide", None),
        ),
        check_vma=False,
    )
```

profile of v0, /device:TPU:24, one launch (start us, length us, event | category | flops | bytes accessed | tf_op | source)
XLA Modules:
  0.0 527.8 jit_solution(5221411180850742156)
XLA Ops:
  10.2 16.4 %all-to-all-start = ((s32[64,1,1]{2,1,0:T(1,128)}), s32[64,1,1]{2,1,0:T(1,128)S(1)}, u32[]{:S(2)}, u32[]{:S(2)}) async-start(s32[64,1,1]{2,1,0:T(1,128)} %copy.172), calls=%async_computation | async-start | bytes 65536 | tf_op jit(solution)/shard_map/all_to_all | solution.py:92
  31.1 1.2 reshape.276
  32.3 3.5 all-to-all-done
  35.8 9.2 %all-to-all-start.1 = ((bf16[64,2,2048]{2,1,0:T(2,128)(2,1)}), bf16[64,2,2048]{2,1,0:T(2,128)(2,1)S(1)}, u32[]{:S(2)}, u32[]{:S(2)}) async-start(bf16[64,2,2048]{2,1,0:T(2,128)(2,1)} %reshape.276), calls=%async_computation.1 | async-start | bytes 1048576 | tf_op jit(solution)/shard_map/all_to_all | solution.py:91
  45.1 1.3 collective-permute-start.5
  46.4 3.0 collective-permute-start.4
  49.4 52.7 %all-gather = bf16[64,54,128]{2,1,0:T(8,128)(2,1)S(1)} all-gather(bf16[1,54,128]{2,1,0:T(8,128)(2,1)S(1)} %bitcast.138), channel_id=1, replica_groups=mesh['wide'=64,'rows'=8] {'wide'}, dimensions={0}, use_global_device_ids=true | all-gather | bytes 898560 | tf_op jit(solution)/shard_map/all_gather | solution.py:105
  102.1 48.3 %all-gather.1 = bf16[64,54,128]{2,1,0:T(8,128)(2,1)S(1)} all-gather(bf16[1,54,128]{2,1,0:T(8,128)(2,1)S(1)} %bitcast.139), channel_id=1, replica_groups=mesh['wide'=64,'rows'=8] {'wide'}, dimensions={0}, use_global_device_ids=true | all-gather | bytes 898560 | tf_op jit(solution)/shard_map/all_gather | solution.py:106
  150.4 1.2 reshape.194
  151.8 1.2 reduce
  153.5 1.2 convolution_select_fusion.1
  156.0 1.3 collective-permute-start.1
  157.3 3.0 collective-permute-start
  162.8 1.3 collective-permute-start.7
  164.1 3.8 collective-permute-start.6
  168.0 1.3 collective-permute-start.3
  169.3 5.0 collective-permute-start.2
  174.5 3.5 multiply_convert_fusion.1
  178.4 1.2 convolution_select_fusion
  182.0 3.5 multiply_convert_fusion
  185.6 74.2 %all-reduce.10.cloned.1.call-done = (bf16[3456,128]{1,0:T(8,128)(2,1)}, bf16[3456,128]{1,0:T(8,128)(2,1)}) async-done(((bf16[3456,128]{1,0:T(8,128)(2,1)}, bf16[3456,128]{1,0:T(8,128)(2,1)}), (bf16[3456,128]{1,0:T(8,128)(2,1)}, bf16[3456,128]{1,0:T(8,128)(2,1)})) %all-reduce.10.cloned.1.call-update) | async-done | bytes 1769488 | tf_op jit(solution)/shard_map/psum | solution.py:133
  259.7 1.4 convert_element_type.113
  261.3 162.5 %fusion.84 = (f32[64,128]{1,0:T(8,128)}, f32[64,128]{1,0:T(8,128)}) fusion(f32[3456,128]{1,0:T(8,128)S(1)} %convert_element_type.113, f32[3456,128]{1,0:T(8,128)S(1)} %convert_element_type.116), kind=kCustom, calls=%all-reduce-scatter.2 | all-reduce-scatter fusion | flops 1048577 | bytes 3606528
  423.8 1.3 collective-permute-start.16
  425.1 1.3 collective-permute-start.15
  426.4 4.0 collective-permute-start.14
  431.2 11.2 %collective-permute-start.13 = (f32[64,128]{1,0:T(8,128)}, f32[64,128]{1,0:T(8,128)S(1)}, u32[]{:S(2)}, u32[]{:S(2)}) collective-permute-start(f32[64,128]{1,0:T(8,128)} %get-tuple-element.28), channel_id=1, source_target_pairs={{0,48},{8,56},{16,64},{24,72},{32,80},{40,88},{48,96},{56,104},{64... | collective-permute-start | bytes 98312
  442.4 2.7 collective-permute-start.17
  445.1 1.5 collective-permute-done.17
  446.6 4.9 collective-permute-start.12
  451.6 9.5 %collective-permute-start.11 = (f32[64,128]{1,0:T(8,128)}, f32[64,128]{1,0:T(8,128)S(1)}, u32[]{:S(2)}, u32[]{:S(2)}) collective-permute-start(f32[64,128]{1,0:T(8,128)} %get-tuple-element.28), channel_id=1, source_target_pairs={{0,32},{8,40},{16,48},{24,56},{32,64},{40,72},{48,80},{56,88},{64,... | collective-permute-start | bytes 98312
  461.1 3.2 collective-permute-start.10
  464.3 7.9 %collective-permute-start.9 = (f32[64,128]{1,0:T(8,128)}, f32[64,128]{1,0:T(8,128)S(1)}, u32[]{:S(2)}, u32[]{:S(2)}) collective-permute-start(f32[64,128]{1,0:T(8,128)} %get-tuple-element.28), channel_id=1, source_target_pairs={{0,16},{8,24},{16,32},{24,40},{32,48},{40,56},{48,64},{56,72},{64,... | collective-permute-start | bytes 98312
  472.2 1.9 collective-permute-start.8
  474.2 1.3 collective-permute-start.26
  475.5 3.5 collective-permute-start.25
  479.0 3.4 collective-permute-start.24
  482.4 3.1 collective-permute-start.23
  486.3 4.0 collective-permute-start.27
  490.4 1.3 dynamic-slice.6
  492.3 2.3 concatenate.49
  494.6 1.3 collective-permute-start.22
  495.9 7.8 %collective-permute-start.21 = (f32[64,128]{1,0:T(8,128)}, f32[64,128]{1,0:T(8,128)S(1)}, u32[]{:S(2)}, u32[]{:S(2)}) collective-permute-start(f32[64,128]{1,0:T(8,128)} %get-tuple-element.29), channel_id=1, source_target_pairs={{0,32},{8,40},{16,48},{24,56},{32,64},{40,72},{48,80},{56,88},{64,... | collective-permute-start | bytes 98312
  503.7 2.5 collective-permute-start.20
  506.2 5.9 %collective-permute-start.19 = (f32[64,128]{1,0:T(8,128)}, f32[64,128]{1,0:T(8,128)S(1)}, u32[]{:S(2)}, u32[]{:S(2)}) collective-permute-start(f32[64,128]{1,0:T(8,128)} %get-tuple-element.29), channel_id=1, source_target_pairs={{0,16},{8,24},{16,32},{24,40},{32,48},{40,56},{48,64},{56,72},{64,... | collective-permute-start | bytes 98312
  512.1 1.9 collective-permute-start.18
  514.6 3.4 collective-permute-done.18
  518.1 2.2 concatenate.50
  (118 shorter events, 17.1 us)
Async XLA Ops:
  10.2 25.6 %all-to-all-start = ((s32[64,1,1]{2,1,0:T(1,128)}), s32[64,1,1]{2,1,0:T(1,128)S(1)}, u32[]{:S(2)}, u32[]{:S(2)}) async-start(s32[64,1,1]{2,1,0:T(1,128)} %copy.172), calls=%async_computation | async-start | bytes 65536 | tf_op jit(solution)/shard_map/all_to_all | solution.py:92
  29.6 19.8 %copy-start.3 = (bf16[54,128]{1,0:T(8,128)(2,1)S(1)}, bf16[54,128]{1,0:T(8,128)(2,1)}, u32[]{:S(2)}) copy-start(bf16[54,128]{1,0:T(8,128)(2,1)} %param.12) | copy-start | bytes 41476
  31.1 71.0 %copy-start.4 = (bf16[54,128]{1,0:T(8,128)(2,1)S(1)}, bf16[54,128]{1,0:T(8,128)(2,1)}, u32[]{:S(2)}) copy-start(bf16[54,128]{1,0:T(8,128)(2,1)} %param.13) | copy-start | bytes 41476
  35.8 118.8 %all-to-all-start.1 = ((bf16[64,2,2048]{2,1,0:T(2,128)(2,1)}), bf16[64,2,2048]{2,1,0:T(2,128)(2,1)S(1)}, u32[]{:S(2)}, u32[]{:S(2)}) async-start(bf16[64,2,2048]{2,1,0:T(2,128)(2,1)} %reshape.276), calls=%async_computation.1 | async-start | bytes 1048576 | tf_op jit(solution)/shard_map/all_to_all | solution.py:91
  45.0 214.7 %all-reduce.10.cloned.1.call-start = ((), (), s32[]{:S(2)}) async-start(), calls=%async_computation.2 | async-start | bytes 3538944 | tf_op jit(solution)/shard_map/psum | solution.py:133
  45.1 107.9 %collective-permute-start.5 = (bf16[5,1,32,128]{3,2,1,0:T(8,128)(2,1)S(1)}, bf16[5,1,32,128]{3,2,1,0:T(8,128)(2,1)S(1)}, u32[]{:S(2)}, u32[]{:S(2)}) collective-permute-start(bf16[5,1,32,128]{3,2,1,0:T(8,128)(2,1)S(1)} %get-tuple-element.44), channel_id=1, source_target_pairs={{1,0},{2,1},{3,2},{4,3},{5,4},{6,5},{7,6},{9,8},{10,9},{11,10},{12... | collective-permute-start | bytes 122888 | tf_op jit(solution)/shard_map/ppermute | solution.py:16
  46.4 106.6 %collective-permute-start.4 = (bf16[5,1,32,128]{3,2,1,0:T(8,128)(2,1)S(1)}, bf16[5,1,32,128]{3,2,1,0:T(8,128)(2,1)S(1)}, u32[]{:S(2)}, u32[]{:S(2)}) collective-permute-start(bf16[5,1,32,128]{3,2,1,0:T(8,128)(2,1)S(1)} %get-tuple-element.43), channel_id=1, source_target_pairs={{0,1},{1,2},{2,3},{3,4},{4,5},{5,6},{6,7},{8,9},{9,10},{10,11},{11... | collective-permute-start | bytes 122888 | tf_op jit(solution)/shard_map/ppermute | solution.py:13
  151.7 1.7 copy-start.5
  156.0 4.6 collective-permute-start.1
  157.3 3.9 collective-permute-start
  160.5 1.2 copy-start
  162.8 15.1 %collective-permute-start.7 = (bf16[5,1,32,128]{3,2,1,0:T(8,128)(2,1)S(1)}, bf16[5,1,32,128]{3,2,1,0:T(8,128)(2,1)S(1)}, u32[]{:S(2)}, u32[]{:S(2)}) collective-permute-start(bf16[5,1,32,128]{3,2,1,0:T(8,128)(2,1)S(1)} %get-tuple-element.40), channel_id=1, source_target_pairs={{1,0},{2,1},{3,2},{4,3},{5,4},{6,5},{7,6},{9,8},{10,9},{11,10},{12... | collective-permute-start | bytes 122888 | tf_op jit(solution)/shard_map/ppermute | solution.py:16
  164.1 13.8 %collective-permute-start.6 = (bf16[5,1,32,128]{3,2,1,0:T(8,128)(2,1)S(1)}, bf16[5,1,32,128]{3,2,1,0:T(8,128)(2,1)S(1)}, u32[]{:S(2)}, u32[]{:S(2)}) collective-permute-start(bf16[5,1,32,128]{3,2,1,0:T(8,128)(2,1)S(1)} %get-tuple-element.39), channel_id=1, source_target_pairs={{0,1},{1,2},{2,3},{3,4},{4,5},{5,6},{6,7},{8,9},{9,10},{10,11},{11... | collective-permute-start | bytes 122888 | tf_op jit(solution)/shard_map/ppermute | solution.py:13
  168.0 11.9 %collective-permute-start.3 = (bf16[5,1,32,128]{3,2,1,0:T(8,128)(2,1)S(1)}, bf16[5,1,32,128]{3,2,1,0:T(8,128)(2,1)S(1)}, u32[]{:S(2)}, u32[]{:S(2)}) collective-permute-start(bf16[5,1,32,128]{3,2,1,0:T(8,128)(2,1)S(1)} %get-tuple-element.46), channel_id=1, source_target_pairs={{1,0},{2,1},{3,2},{4,3},{5,4},{6,5},{7,6},{9,8},{10,9},{11,10},{12... | collective-permute-start | bytes 122888 | tf_op jit(solution)/shard_map/ppermute | solution.py:16
  169.3 10.6 %collective-permute-start.2 = (bf16[5,1,32,128]{3,2,1,0:T(8,128)(2,1)S(1)}, bf16[5,1,32,128]{3,2,1,0:T(8,128)(2,1)S(1)}, u32[]{:S(2)}, u32[]{:S(2)}) collective-permute-start(bf16[5,1,32,128]{3,2,1,0:T(8,128)(2,1)S(1)} %get-tuple-element.45), channel_id=1, source_target_pairs={{0,1},{1,2},{2,3},{3,4},{4,5},{5,6},{6,7},{8,9},{9,10},{10,11},{11... | collective-permute-start | bytes 122888 | tf_op jit(solution)/shard_map/ppermute | solution.py:13
  180.2 1.0 copy-start.2
  259.7 1.4 copy-start.1
  423.8 27.8 %collective-permute-start.16 = (f32[64,128]{1,0:T(8,128)}, f32[64,128]{1,0:T(8,128)S(1)}, u32[]{:S(2)}, u32[]{:S(2)}) collective-permute-start(f32[64,128]{1,0:T(8,128)} %get-tuple-element.28), channel_id=1, source_target_pairs={{0,72},{8,80},{16,88},{24,96},{32,104},{40,112},{48,120},{56,128},... | collective-permute-start | bytes 98312
  425.1 36.0 %collective-permute-start.15 = (f32[64,128]{1,0:T(8,128)}, f32[64,128]{1,0:T(8,128)S(1)}, u32[]{:S(2)}, u32[]{:S(2)}) collective-permute-start(f32[64,128]{1,0:T(8,128)} %get-tuple-element.28), channel_id=1, source_target_pairs={{0,64},{8,72},{16,80},{24,88},{32,96},{40,104},{48,112},{56,120},{... | collective-permute-start | bytes 98312
  426.4 37.9 %collective-permute-start.14 = (f32[64,128]{1,0:T(8,128)}, f32[64,128]{1,0:T(8,128)S(1)}, u32[]{:S(2)}, u32[]{:S(2)}) collective-permute-start(f32[64,128]{1,0:T(8,128)} %get-tuple-element.28), channel_id=1, source_target_pairs={{0,56},{8,64},{16,72},{24,80},{32,88},{40,96},{48,104},{56,112},{6... | collective-permute-start | bytes 98312
  431.2 41.1 %collective-permute-start.13 = (f32[64,128]{1,0:T(8,128)}, f32[64,128]{1,0:T(8,128)S(1)}, u32[]{:S(2)}, u32[]{:S(2)}) collective-permute-start(f32[64,128]{1,0:T(8,128)} %get-tuple-element.28), channel_id=1, source_target_pairs={{0,48},{8,56},{16,64},{24,72},{32,80},{40,88},{48,96},{56,104},{64... | collective-permute-start | bytes 98312
  442.4 4.2 collective-permute-start.17
  446.6 27.5 %collective-permute-start.12 = (f32[64,128]{1,0:T(8,128)}, f32[64,128]{1,0:T(8,128)S(1)}, u32[]{:S(2)}, u32[]{:S(2)}) collective-permute-start(f32[64,128]{1,0:T(8,128)} %get-tuple-element.28), channel_id=1, source_target_pairs={{0,40},{8,48},{16,56},{24,64},{32,72},{40,80},{48,88},{56,96},{64,... | collective-permute-start | bytes 98312
  451.6 23.9 %collective-permute-start.11 = (f32[64,128]{1,0:T(8,128)}, f32[64,128]{1,0:T(8,128)S(1)}, u32[]{:S(2)}, u32[]{:S(2)}) collective-permute-start(f32[64,128]{1,0:T(8,128)} %get-tuple-element.28), channel_id=1, source_target_pairs={{0,32},{8,40},{16,48},{24,56},{32,64},{40,72},{48,80},{56,88},{64,... | collective-permute-start | bytes 98312
  461.1 17.9 %collective-permute-start.10 = (f32[64,128]{1,0:T(8,128)}, f32[64,128]{1,0:T(8,128)S(1)}, u32[]{:S(2)}, u32[]{:S(2)}) collective-permute-start(f32[64,128]{1,0:T(8,128)} %get-tuple-element.28), channel_id=1, source_target_pairs={{0,24},{8,32},{16,40},{24,48},{32,56},{40,64},{48,72},{56,80},{64,... | collective-permute-start | bytes 98312
  464.3 18.1 %collective-permute-start.9 = (f32[64,128]{1,0:T(8,128)}, f32[64,128]{1,0:T(8,128)S(1)}, u32[]{:S(2)}, u32[]{:S(2)}) collective-permute-start(f32[64,128]{1,0:T(8,128)} %get-tuple-element.28), channel_id=1, source_target_pairs={{0,16},{8,24},{16,32},{24,40},{32,48},{40,56},{48,64},{56,72},{64,... | collective-permute-start | bytes 98312
  472.2 14.1 %collective-permute-start.8 = (f32[64,128]{1,0:T(8,128)}, f32[64,128]{1,0:T(8,128)S(1)}, u32[]{:S(2)}, u32[]{:S(2)}) collective-permute-start(f32[64,128]{1,0:T(8,128)} %get-tuple-element.28), channel_id=1, source_target_pairs={{0,8},{8,16},{16,24},{24,32},{32,40},{40,48},{48,56},{56,64},{64,7... | collective-permute-start | bytes 98312
  474.2 21.7 %collective-permute-start.26 = (f32[64,128]{1,0:T(8,128)}, f32[64,128]{1,0:T(8,128)S(1)}, u32[]{:S(2)}, u32[]{:S(2)}) collective-permute-start(f32[64,128]{1,0:T(8,128)} %get-tuple-element.29), channel_id=1, source_target_pairs={{0,72},{8,80},{16,88},{24,96},{32,104},{40,112},{48,120},{56,128},... | collective-permute-start | bytes 98312
  475.5 28.2 %collective-permute-start.25 = (f32[64,128]{1,0:T(8,128)}, f32[64,128]{1,0:T(8,128)S(1)}, u32[]{:S(2)}, u32[]{:S(2)}) collective-permute-start(f32[64,128]{1,0:T(8,128)} %get-tuple-element.29), channel_id=1, source_target_pairs={{0,64},{8,72},{16,80},{24,88},{32,96},{40,104},{48,112},{56,120},{... | collective-permute-start | bytes 98312
  479.0 27.1 %collective-permute-start.24 = (f32[64,128]{1,0:T(8,128)}, f32[64,128]{1,0:T(8,128)S(1)}, u32[]{:S(2)}, u32[]{:S(2)}) collective-permute-start(f32[64,128]{1,0:T(8,128)} %get-tuple-element.29), channel_id=1, source_target_pairs={{0,56},{8,64},{16,72},{24,80},{32,88},{40,96},{48,104},{56,112},{6... | collective-permute-start | bytes 98312
  482.4 29.6 %collective-permute-start.23 = (f32[64,128]{1,0:T(8,128)}, f32[64,128]{1,0:T(8,128)S(1)}, u32[]{:S(2)}, u32[]{:S(2)}) collective-permute-start(f32[64,128]{1,0:T(8,128)} %get-tuple-element.29), channel_id=1, source_target_pairs={{0,48},{8,56},{16,64},{24,72},{32,80},{40,88},{48,96},{56,104},{64... | collective-permute-start | bytes 98312
  486.3 8.3 %collective-permute-start.27 = (f32[54,128]{1,0:T(8,128)S(1)}, f32[54,128]{1,0:T(8,128)S(1)}, u32[]{:S(2)}, u32[]{:S(2)}) collective-permute-start(f32[54,128]{1,0:T(8,128)S(1)} %slice.136), channel_id=1, source_target_pairs={{0,80},{8,88},{16,96},{24,104},{32,112},{40,120},{48,128},{56,136}... | collective-permute-start | bytes 82952
  494.6 20.0 %collective-permute-start.22 = (f32[64,128]{1,0:T(8,128)}, f32[64,128]{1,0:T(8,128)S(1)}, u32[]{:S(2)}, u32[]{:S(2)}) collective-permute-start(f32[64,128]{1,0:T(8,128)} %get-tuple-element.29), channel_id=1, source_target_pairs={{0,40},{8,48},{16,56},{24,64},{32,72},{40,80},{48,88},{56,96},{64,... | collective-permute-start | bytes 98312
  495.9 18.7 %collective-permute-start.21 = (f32[64,128]{1,0:T(8,128)}, f32[64,128]{1,0:T(8,128)S(1)}, u32[]{:S(2)}, u32[]{:S(2)}) collective-permute-start(f32[64,128]{1,0:T(8,128)} %get-tuple-element.29), channel_id=1, source_target_pairs={{0,32},{8,40},{16,48},{24,56},{32,64},{40,72},{48,80},{56,88},{64,... | collective-permute-start | bytes 98312
  503.7 10.9 %collective-permute-start.20 = (f32[64,128]{1,0:T(8,128)}, f32[64,128]{1,0:T(8,128)S(1)}, u32[]{:S(2)}, u32[]{:S(2)}) collective-permute-start(f32[64,128]{1,0:T(8,128)} %get-tuple-element.29), channel_id=1, source_target_pairs={{0,24},{8,32},{16,40},{24,48},{32,56},{40,64},{48,72},{56,80},{64,... | collective-permute-start | bytes 98312
  506.2 8.4 %collective-permute-start.19 = (f32[64,128]{1,0:T(8,128)}, f32[64,128]{1,0:T(8,128)S(1)}, u32[]{:S(2)}, u32[]{:S(2)}) collective-permute-start(f32[64,128]{1,0:T(8,128)} %get-tuple-element.29), channel_id=1, source_target_pairs={{0,16},{8,24},{16,32},{24,40},{32,48},{40,56},{48,64},{56,72},{64,... | collective-permute-start | bytes 98312
  512.1 6.0 %collective-permute-start.18 = (f32[64,128]{1,0:T(8,128)}, f32[64,128]{1,0:T(8,128)S(1)}, u32[]{:S(2)}, u32[]{:S(2)}) collective-permute-start(f32[64,128]{1,0:T(8,128)} %get-tuple-element.29), channel_id=1, source_target_pairs={{0,8},{8,16},{16,24},{24,32},{32,40},{40,48},{48,56},{56,64},{64,7... | collective-permute-start | bytes 98312
Sparse Core Ops, SparseCore 0:
  185.7 74.0 all-reduce.9
where the time goes:
time: 529 us; the launch traced here: 528 us
  blocking collectives  263 us (50%)
  starting transfers between devices  128 us (24%)
  waiting for transfers between devices  83.3 us (16%)
  between operations  16.3 us (3%)
  local copies, waits for them, and re-layouts  16.2 us (3%)
  matrix products  12.2 us (2%)
  other arithmetic  8.08 us (2%)
    unnamed x1, blocking collectives  163 us
    unnamed x20, starting transfers between devices  82.6 us
    psum x1, waiting for transfers between devices, body(): lax.psum(weight_first.astype(jnp.bfloat16), 'rows').astype(jnp.float32)  74.2 us
    all_gather x1, blocking collectives, body(): lax.all_gather(w_first, 'wide', axis=0, tiled=True)  52.7 us
    all_gather x1, blocking collectives, body(): lax.all_gather(w_second, 'wide', axis=0, tiled=True)  48.3 us
    all_to_all x1, starting transfers between devices, body(): lax.all_to_all(labels, 'wide', split_axis=0, concat_axis=0, tiled=True)  16.4 us
    ppermute x4, starting transfers between devices, with_halo(): lax.ppermute(lax.slice_in_dim(block, block.shape[dim] - width, None, axis...  14.9 us
    unnamed x33, local copies, waits for them, and re-layouts  12.1 us
  transfers between devices with their start and end apart: 31, of which 5 were waited for; matrix products, arithmetic and copies ran while one was open for 4% of the time, Pallas kernels for 0%

commit v1 on v0

--- a/solution.py
+++ b/solution.py
@@ -130,7 +130,9 @@
     weight_first = weight_first * scale
     weight_second = weight_second * scale
     total_first, total_second = (
-        lax.psum(weight_first.astype(jnp.bfloat16), "rows").astype(jnp.float32),
+        jnp.sum(lax.all_gather(weight_first.astype(jnp.bfloat16), "rows"), axis=0).astype(
+            jnp.float32
+        ),
         lax.psum(weight_second.astype(jnp.bfloat16), "rows").astype(jnp.float32),
     )
     share_first, share_second = (

time: 529 us -> 580 us (1.096)
  waiting for transfers between devices: 83.3 us -> 127 us
  other arithmetic: 8.08 us -> 14.3 us
    all_gather x0 -> x1, waiting for transfers between devices: none -> 49.5 us  [body(): lax.all_gather(weight_first.astype(jnp.bfloat16), 'rows')]
    psum x1, waiting for transfers between devices: 74.2 us -> 68.2 us  [body(): lax.psum(weight_second.astype(jnp.bfloat16), 'rows').astype(jnp.float32)]
    unnamed x33 -> x31, local copies, waits for them, and re-layouts: 12.1 us -> 12 us
  transfers between devices with their start and end apart: 31 -> 32, of which waited for: 5 -> 6; matrix products, arithmetic and copies ran while one was open for 4% -> 4% of each run, Pallas kernels for 0% -> 0%
where the time goes in v1:
time: 580 us; the launch traced here: 578 us
  blocking collectives  263 us (45%)
  starting transfers between devices  129 us (22%)
  waiting for transfers between devices  127 us (22%)
  between operations  16.3 us (3%)
  local copies, waits for them, and re-layouts  16.1 us (3%)
  other arithmetic  14.3 us (2%)
  matrix products  12.2 us (2%)
    unnamed x1, blocking collectives  162 us
    unnamed x20, starting transfers between devices  83.5 us
    psum x1, waiting for transfers between devices, body(): lax.psum(weight_second.astype(jnp.bfloat16), 'rows').astype(jnp.float32)  68.2 us
    all_gather x1, blocking collectives, body(): lax.all_gather(w_first, 'wide', axis=0, tiled=True)  52.7 us
    all_gather x1, waiting for transfers between devices, body(): lax.all_gather(weight_first.astype(jnp.bfloat16), 'rows')  49.5 us
    all_gather x1, blocking collectives, body(): lax.all_gather(w_second, 'wide', axis=0, tiled=True)  48.3 us
    all_to_all x1, starting transfers between devices, body(): lax.all_to_all(labels, 'wide', split_axis=0, concat_axis=0, tiled=True)  16.4 us
    ppermute x4, starting transfers between devices, with_halo(): lax.ppermute(lax.slice_in_dim(block, block.shape[dim] - width, None, axis...  14.9 us
  transfers between devices with their start and end apart: 32, of which 6 were waited for; matrix products, arithmetic and copies ran while one was open for 4% of the time, Pallas kernels for 0%

profile of v1, /device:TPU:24, one launch (start us, length us, event | category | flops | bytes accessed | tf_op | source)
XLA Modules:
  0.0 578.1 jit_solution(15291778664874072127)
XLA Ops:
  10.2 16.4 %all-to-all-start = ((s32[64,1,1]{2,1,0:T(1,128)}), s32[64,1,1]{2,1,0:T(1,128)S(1)}, u32[]{:S(2)}, u32[]{:S(2)}) async-start(s32[64,1,1]{2,1,0:T(1,128)} %copy.172), calls=%async_computation | async-start | bytes 65536 | tf_op jit(solution)/shard_map/all_to_all | solution.py:92
  32.3 3.5 all-to-all-done
  35.8 9.2 %all-to-all-start.1 = ((bf16[64,2,2048]{2,1,0:T(2,128)(2,1)}), bf16[64,2,2048]{2,1,0:T(2,128)(2,1)S(1)}, u32[]{:S(2)}, u32[]{:S(2)}) async-start(bf16[64,2,2048]{2,1,0:T(2,128)(2,1)} %reshape.289), calls=%async_computation.1 | async-start | bytes 1048576 | tf_op jit(solution)/shard_map/all_to_all | solution.py:91
  45.1 1.3 collective-permute-start.5
  46.4 3.0 collective-permute-start.4
  49.4 52.7 %all-gather = bf16[64,54,128]{2,1,0:T(8,128)(2,1)S(1)} all-gather(bf16[1,54,128]{2,1,0:T(8,128)(2,1)S(1)} %bitcast.138), channel_id=1, replica_groups=mesh['wide'=64,'rows'=8] {'wide'}, dimensions={0}, use_global_device_ids=true | all-gather | bytes 898560 | tf_op jit(solution)/shard_map/all_gather | solution.py:105
  102.1 48.3 %all-gather.1 = bf16[64,54,128]{2,1,0:T(8,128)(2,1)S(1)} all-gather(bf16[1,54,128]{2,1,0:T(8,128)(2,1)S(1)} %bitcast.139), channel_id=1, replica_groups=mesh['wide'=64,'rows'=8] {'wide'}, dimensions={0}, use_global_device_ids=true | all-gather | bytes 898560 | tf_op jit(solution)/shard_map/all_gather | solution.py:106
  151.8 1.2 reduce.1
  153.5 1.2 convolution_select_fusion.1
  156.0 1.3 collective-permute-start.1
  157.3 3.0 collective-permute-start
  162.9 1.3 collective-permute-start.7
  164.2 3.8 collective-permute-start.6
  168.0 1.3 collective-permute-start.3
  169.3 5.0 collective-permute-start.2
  178.6 3.5 multiply_convert_fusion
  182.1 3.5 multiply_convert_fusion.1
  185.7 68.2 %all-reduce.9.cloned.1.call-done = bf16[3456,128]{1,0:T(8,128)(2,1)} async-done(((bf16[3456,128]{1,0:T(8,128)(2,1)}), bf16[3456,128]{1,0:T(8,128)(2,1)}) %all-reduce.9.cloned.1.call-update) | async-done | bytes 884752 | tf_op jit(solution)/shard_map/psum | solution.py:136
  253.8 1.3 convert_element_type.125
  255.1 49.5 %all-gather.4.cloned.1.call-done = bf16[8,3456,128]{2,1,0:T(8,128)(2,1)} async-done(((bf16[1,3456,128]{2,1,0:T(8,128)(2,1)}), bf16[8,3456,128]{2,1,0:T(8,128)(2,1)}) %all-gather.4.cloned.1.call-update) | async-done | bytes 7077904 | tf_op jit(solution)/shard_map/all_gather | solution.py:133
  304.6 5.2 reduce_sum.32
  309.8 1.3 convert_element_type.122
  311.1 162.1 %fusion.84 = (f32[64,128]{1,0:T(8,128)}, f32[64,128]{1,0:T(8,128)}) fusion(f32[3456,128]{1,0:T(8,128)S(1)} %convert_element_type.122, f32[3456,128]{1,0:T(8,128)S(1)} %convert_element_type.125), kind=kCustom, calls=%all-reduce-scatter.2 | all-reduce-scatter fusion | flops 1048577 | bytes 3606528
  473.2 1.3 collective-permute-start.16
  474.5 1.3 collective-permute-start.15
  475.8 3.6 collective-permute-start.14
  480.2 12.2 %collective-permute-start.13 = (f32[64,128]{1,0:T(8,128)}, f32[64,128]{1,0:T(8,128)S(1)}, u32[]{:S(2)}, u32[]{:S(2)}) collective-permute-start(f32[64,128]{1,0:T(8,128)} %get-tuple-element.26), channel_id=1, source_target_pairs={{0,48},{8,56},{16,64},{24,72},{32,80},{40,88},{48,96},{56,104},{64... | collective-permute-start | bytes 98312
  492.4 1.7 collective-permute-start.17
  494.1 1.5 collective-permute-done.17
  495.7 4.9 collective-permute-start.12
  500.6 9.3 %collective-permute-start.11 = (f32[64,128]{1,0:T(8,128)}, f32[64,128]{1,0:T(8,128)S(1)}, u32[]{:S(2)}, u32[]{:S(2)}) collective-permute-start(f32[64,128]{1,0:T(8,128)} %get-tuple-element.26), channel_id=1, source_target_pairs={{0,32},{8,40},{16,48},{24,56},{32,64},{40,72},{48,80},{56,88},{64,... | collective-permute-start | bytes 98312
  509.9 3.4 collective-permute-start.10
  513.3 7.9 %collective-permute-start.9 = (f32[64,128]{1,0:T(8,128)}, f32[64,128]{1,0:T(8,128)S(1)}, u32[]{:S(2)}, u32[]{:S(2)}) collective-permute-start(f32[64,128]{1,0:T(8,128)} %get-tuple-element.26), channel_id=1, source_target_pairs={{0,16},{8,24},{16,32},{24,40},{32,48},{40,56},{48,64},{56,72},{64,... | collective-permute-start | bytes 98312
  521.3 1.9 collective-permute-start.8
  523.2 1.3 collective-permute-start.26
  524.5 4.8 collective-permute-start.25
  529.4 3.4 collective-permute-start.24
  532.8 3.1 collective-permute-start.23
  536.7 4.0 collective-permute-start.27
  540.7 1.3 dynamic-slice.6
  542.6 2.3 concatenate.49
  544.9 1.3 collective-permute-start.22
  546.2 7.8 %collective-permute-start.21 = (f32[64,128]{1,0:T(8,128)}, f32[64,128]{1,0:T(8,128)S(1)}, u32[]{:S(2)}, u32[]{:S(2)}) collective-permute-start(f32[64,128]{1,0:T(8,128)} %get-tuple-element.27), channel_id=1, source_target_pairs={{0,32},{8,40},{16,48},{24,56},{32,64},{40,72},{48,80},{56,88},{64,... | collective-permute-start | bytes 98312
  554.0 2.5 collective-permute-start.20
  556.5 5.9 %collective-permute-start.19 = (f32[64,128]{1,0:T(8,128)}, f32[64,128]{1,0:T(8,128)S(1)}, u32[]{:S(2)}, u32[]{:S(2)}) collective-permute-start(f32[64,128]{1,0:T(8,128)} %get-tuple-element.27), channel_id=1, source_target_pairs={{0,16},{8,24},{16,32},{24,40},{32,48},{40,56},{48,64},{56,72},{64,... | collective-permute-start | bytes 98312
  562.4 1.9 collective-permute-start.18
  565.0 3.4 collective-permute-done.18
  568.4 2.2 concatenate.50
  (120 shorter events, 20.5 us)
Async XLA Ops:
  10.2 25.6 %all-to-all-start = ((s32[64,1,1]{2,1,0:T(1,128)}), s32[64,1,1]{2,1,0:T(1,128)S(1)}, u32[]{:S(2)}, u32[]{:S(2)}) async-start(s32[64,1,1]{2,1,0:T(1,128)} %copy.172), calls=%async_computation | async-start | bytes 65536 | tf_op jit(solution)/shard_map/all_to_all | solution.py:92
  29.6 19.8 %copy-start.2 = (bf16[54,128]{1,0:T(8,128)(2,1)S(1)}, bf16[54,128]{1,0:T(8,128)(2,1)}, u32[]{:S(2)}) copy-start(bf16[54,128]{1,0:T(8,128)(2,1)} %param.12) | copy-start | bytes 41476
  31.1 71.0 %copy-start.3 = (bf16[54,128]{1,0:T(8,128)(2,1)S(1)}, bf16[54,128]{1,0:T(8,128)(2,1)}, u32[]{:S(2)}) copy-start(bf16[54,128]{1,0:T(8,128)(2,1)} %param.13) | copy-start | bytes 41476
  35.8 118.9 %all-to-all-start.1 = ((bf16[64,2,2048]{2,1,0:T(2,128)(2,1)}), bf16[64,2,2048]{2,1,0:T(2,128)(2,1)S(1)}, u32[]{:S(2)}, u32[]{:S(2)}) async-start(bf16[64,2,2048]{2,1,0:T(2,128)(2,1)} %reshape.289), calls=%async_computation.1 | async-start | bytes 1048576 | tf_op jit(solution)/shard_map/all_to_all | solution.py:91
  45.0 208.8 %all-reduce.9.cloned.1.call-start = ((), (), s32[]{:S(2)}) async-start(), calls=%async_computation.3 | async-start | bytes 1769472 | tf_op jit(solution)/shard_map/psum | solution.py:136
  45.1 107.9 %collective-permute-start.5 = (bf16[5,1,32,128]{3,2,1,0:T(8,128)(2,1)S(1)}, bf16[5,1,32,128]{3,2,1,0:T(8,128)(2,1)S(1)}, u32[]{:S(2)}, u32[]{:S(2)}) collective-permute-start(bf16[5,1,32,128]{3,2,1,0:T(8,128)(2,1)S(1)} %get-tuple-element.42), channel_id=1, source_target_pairs={{1,0},{2,1},{3,2},{4,3},{5,4},{6,5},{7,6},{9,8},{10,9},{11,10},{12... | collective-permute-start | bytes 122888 | tf_op jit(solution)/shard_map/ppermute | solution.py:16
  46.4 106.6 %collective-permute-start.4 = (bf16[5,1,32,128]{3,2,1,0:T(8,128)(2,1)S(1)}, bf16[5,1,32,128]{3,2,1,0:T(8,128)(2,1)S(1)}, u32[]{:S(2)}, u32[]{:S(2)}) collective-permute-start(bf16[5,1,32,128]{3,2,1,0:T(8,128)(2,1)S(1)} %get-tuple-element.41), channel_id=1, source_target_pairs={{0,1},{1,2},{2,3},{3,4},{4,5},{5,6},{6,7},{8,9},{9,10},{10,11},{11... | collective-permute-start | bytes 122888 | tf_op jit(solution)/shard_map/ppermute | solution.py:13
  151.8 1.7 copy-start.4
  156.0 4.6 collective-permute-start.1
  157.3 3.9 collective-permute-start
  160.5 1.2 copy-start
  162.9 11.6 %collective-permute-start.7 = (bf16[5,1,32,128]{3,2,1,0:T(8,128)(2,1)S(1)}, bf16[5,1,32,128]{3,2,1,0:T(8,128)(2,1)S(1)}, u32[]{:S(2)}, u32[]{:S(2)}) collective-permute-start(bf16[5,1,32,128]{3,2,1,0:T(8,128)(2,1)S(1)} %get-tuple-element.38), channel_id=1, source_target_pairs={{1,0},{2,1},{3,2},{4,3},{5,4},{6,5},{7,6},{9,8},{10,9},{11,10},{12... | collective-permute-start | bytes 122888 | tf_op jit(solution)/shard_map/ppermute | solution.py:16
  164.2 10.3 %collective-permute-start.6 = (bf16[5,1,32,128]{3,2,1,0:T(8,128)(2,1)S(1)}, bf16[5,1,32,128]{3,2,1,0:T(8,128)(2,1)S(1)}, u32[]{:S(2)}, u32[]{:S(2)}) collective-permute-start(bf16[5,1,32,128]{3,2,1,0:T(8,128)(2,1)S(1)} %get-tuple-element.37), channel_id=1, source_target_pairs={{0,1},{1,2},{2,3},{3,4},{4,5},{5,6},{6,7},{8,9},{9,10},{10,11},{11... | collective-permute-start | bytes 122888 | tf_op jit(solution)/shard_map/ppermute | solution.py:13
  168.0 8.4 %collective-permute-start.3 = (bf16[5,1,32,128]{3,2,1,0:T(8,128)(2,1)S(1)}, bf16[5,1,32,128]{3,2,1,0:T(8,128)(2,1)S(1)}, u32[]{:S(2)}, u32[]{:S(2)}) collective-permute-start(bf16[5,1,32,128]{3,2,1,0:T(8,128)(2,1)S(1)} %get-tuple-element.44), channel_id=1, source_target_pairs={{1,0},{2,1},{3,2},{4,3},{5,4},{6,5},{7,6},{9,8},{10,9},{11,10},{12... | collective-permute-start | bytes 122888 | tf_op jit(solution)/shard_map/ppermute | solution.py:16
  169.3 7.1 %collective-permute-start.2 = (bf16[5,1,32,128]{3,2,1,0:T(8,128)(2,1)S(1)}, bf16[5,1,32,128]{3,2,1,0:T(8,128)(2,1)S(1)}, u32[]{:S(2)}, u32[]{:S(2)}) collective-permute-start(bf16[5,1,32,128]{3,2,1,0:T(8,128)(2,1)S(1)} %get-tuple-element.43), channel_id=1, source_target_pairs={{0,1},{1,2},{2,3},{3,4},{4,5},{5,6},{6,7},{8,9},{9,10},{10,11},{11... | collective-permute-start | bytes 122888 | tf_op jit(solution)/shard_map/ppermute | solution.py:13
  176.8 1.0 copy-start.1
  182.1 122.5 %all-gather.4.cloned.1.call-start = ((), (), s32[]{:S(2)}) async-start(), calls=%async_computation.2 | async-start | bytes 7962624 | tf_op jit(solution)/shard_map/all_gather | solution.py:133
  473.2 27.4 %collective-permute-start.16 = (f32[64,128]{1,0:T(8,128)}, f32[64,128]{1,0:T(8,128)S(1)}, u32[]{:S(2)}, u32[]{:S(2)}) collective-permute-start(f32[64,128]{1,0:T(8,128)} %get-tuple-element.26), channel_id=1, source_target_pairs={{0,72},{8,80},{16,88},{24,96},{32,104},{40,112},{48,120},{56,128},... | collective-permute-start | bytes 98312
  474.5 35.4 %collective-permute-start.15 = (f32[64,128]{1,0:T(8,128)}, f32[64,128]{1,0:T(8,128)S(1)}, u32[]{:S(2)}, u32[]{:S(2)}) collective-permute-start(f32[64,128]{1,0:T(8,128)} %get-tuple-element.26), channel_id=1, source_target_pairs={{0,64},{8,72},{16,80},{24,88},{32,96},{40,104},{48,112},{56,120},{... | collective-permute-start | bytes 98312
  475.8 37.5 %collective-permute-start.14 = (f32[64,128]{1,0:T(8,128)}, f32[64,128]{1,0:T(8,128)S(1)}, u32[]{:S(2)}, u32[]{:S(2)}) collective-permute-start(f32[64,128]{1,0:T(8,128)} %get-tuple-element.26), channel_id=1, source_target_pairs={{0,56},{8,64},{16,72},{24,80},{32,88},{40,96},{48,104},{56,112},{6... | collective-permute-start | bytes 98312
  480.2 41.1 %collective-permute-start.13 = (f32[64,128]{1,0:T(8,128)}, f32[64,128]{1,0:T(8,128)S(1)}, u32[]{:S(2)}, u32[]{:S(2)}) collective-permute-start(f32[64,128]{1,0:T(8,128)} %get-tuple-element.26), channel_id=1, source_target_pairs={{0,48},{8,56},{16,64},{24,72},{32,80},{40,88},{48,96},{56,104},{64... | collective-permute-start | bytes 98312
  492.4 3.3 collective-permute-start.17
  495.7 27.5 %collective-permute-start.12 = (f32[64,128]{1,0:T(8,128)}, f32[64,128]{1,0:T(8,128)S(1)}, u32[]{:S(2)}, u32[]{:S(2)}) collective-permute-start(f32[64,128]{1,0:T(8,128)} %get-tuple-element.26), channel_id=1, source_target_pairs={{0,40},{8,48},{16,56},{24,64},{32,72},{40,80},{48,88},{56,96},{64,... | collective-permute-start | bytes 98312
  500.6 23.9 %collective-permute-start.11 = (f32[64,128]{1,0:T(8,128)}, f32[64,128]{1,0:T(8,128)S(1)}, u32[]{:S(2)}, u32[]{:S(2)}) collective-permute-start(f32[64,128]{1,0:T(8,128)} %get-tuple-element.26), channel_id=1, source_target_pairs={{0,32},{8,40},{16,48},{24,56},{32,64},{40,72},{48,80},{56,88},{64,... | collective-permute-start | bytes 98312
  509.9 19.5 %collective-permute-start.10 = (f32[64,128]{1,0:T(8,128)}, f32[64,128]{1,0:T(8,128)S(1)}, u32[]{:S(2)}, u32[]{:S(2)}) collective-permute-start(f32[64,128]{1,0:T(8,128)} %get-tuple-element.26), channel_id=1, source_target_pairs={{0,24},{8,32},{16,40},{24,48},{32,56},{40,64},{48,72},{56,80},{64,... | collective-permute-start | bytes 98312
  513.3 19.4 %collective-permute-start.9 = (f32[64,128]{1,0:T(8,128)}, f32[64,128]{1,0:T(8,128)S(1)}, u32[]{:S(2)}, u32[]{:S(2)}) collective-permute-start(f32[64,128]{1,0:T(8,128)} %get-tuple-element.26), channel_id=1, source_target_pairs={{0,16},{8,24},{16,32},{24,40},{32,48},{40,56},{48,64},{56,72},{64,... | collective-permute-start | bytes 98312
  521.3 15.4 %collective-permute-start.8 = (f32[64,128]{1,0:T(8,128)}, f32[64,128]{1,0:T(8,128)S(1)}, u32[]{:S(2)}, u32[]{:S(2)}) collective-permute-start(f32[64,128]{1,0:T(8,128)} %get-tuple-element.26), channel_id=1, source_target_pairs={{0,8},{8,16},{16,24},{24,32},{32,40},{40,48},{48,56},{56,64},{64,7... | collective-permute-start | bytes 98312
  523.2 23.0 %collective-permute-start.26 = (f32[64,128]{1,0:T(8,128)}, f32[64,128]{1,0:T(8,128)S(1)}, u32[]{:S(2)}, u32[]{:S(2)}) collective-permute-start(f32[64,128]{1,0:T(8,128)} %get-tuple-element.27), channel_id=1, source_target_pairs={{0,72},{8,80},{16,88},{24,96},{32,104},{40,112},{48,120},{56,128},... | collective-permute-start | bytes 98312
  524.5 29.5 %collective-permute-start.25 = (f32[64,128]{1,0:T(8,128)}, f32[64,128]{1,0:T(8,128)S(1)}, u32[]{:S(2)}, u32[]{:S(2)}) collective-permute-start(f32[64,128]{1,0:T(8,128)} %get-tuple-element.27), channel_id=1, source_target_pairs={{0,64},{8,72},{16,80},{24,88},{32,96},{40,104},{48,112},{56,120},{... | collective-permute-start | bytes 98312
  529.4 27.1 %collective-permute-start.24 = (f32[64,128]{1,0:T(8,128)}, f32[64,128]{1,0:T(8,128)S(1)}, u32[]{:S(2)}, u32[]{:S(2)}) collective-permute-start(f32[64,128]{1,0:T(8,128)} %get-tuple-element.27), channel_id=1, source_target_pairs={{0,56},{8,64},{16,72},{24,80},{32,88},{40,96},{48,104},{56,112},{6... | collective-permute-start | bytes 98312
  532.8 29.6 %collective-permute-start.23 = (f32[64,128]{1,0:T(8,128)}, f32[64,128]{1,0:T(8,128)S(1)}, u32[]{:S(2)}, u32[]{:S(2)}) collective-permute-start(f32[64,128]{1,0:T(8,128)} %get-tuple-element.27), channel_id=1, source_target_pairs={{0,48},{8,56},{16,64},{24,72},{32,80},{40,88},{48,96},{56,104},{64... | collective-permute-start | bytes 98312
  536.7 8.3 %collective-permute-start.27 = (f32[54,128]{1,0:T(8,128)S(1)}, f32[54,128]{1,0:T(8,128)S(1)}, u32[]{:S(2)}, u32[]{:S(2)}) collective-permute-start(f32[54,128]{1,0:T(8,128)S(1)} %slice.136), channel_id=1, source_target_pairs={{0,80},{8,88},{16,96},{24,104},{32,112},{40,120},{48,128},{56,136}... | collective-permute-start | bytes 82952
  544.9 20.0 %collective-permute-start.22 = (f32[64,128]{1,0:T(8,128)}, f32[64,128]{1,0:T(8,128)S(1)}, u32[]{:S(2)}, u32[]{:S(2)}) collective-permute-start(f32[64,128]{1,0:T(8,128)} %get-tuple-element.27), channel_id=1, source_target_pairs={{0,40},{8,48},{16,56},{24,64},{32,72},{40,80},{48,88},{56,96},{64,... | collective-permute-start | bytes 98312
  546.2 18.7 %collective-permute-start.21 = (f32[64,128]{1,0:T(8,128)}, f32[64,128]{1,0:T(8,128)S(1)}, u32[]{:S(2)}, u32[]{:S(2)}) collective-permute-start(f32[64,128]{1,0:T(8,128)} %get-tuple-element.27), channel_id=1, source_target_pairs={{0,32},{8,40},{16,48},{24,56},{32,64},{40,72},{48,80},{56,88},{64,... | collective-permute-start | bytes 98312
  554.0 10.9 %collective-permute-start.20 = (f32[64,128]{1,0:T(8,128)}, f32[64,128]{1,0:T(8,128)S(1)}, u32[]{:S(2)}, u32[]{:S(2)}) collective-permute-start(f32[64,128]{1,0:T(8,128)} %get-tuple-element.27), channel_id=1, source_target_pairs={{0,24},{8,32},{16,40},{24,48},{32,56},{40,64},{48,72},{56,80},{64,... | collective-permute-start | bytes 98312
  556.5 8.4 %collective-permute-start.19 = (f32[64,128]{1,0:T(8,128)}, f32[64,128]{1,0:T(8,128)S(1)}, u32[]{:S(2)}, u32[]{:S(2)}) collective-permute-start(f32[64,128]{1,0:T(8,128)} %get-tuple-element.27), channel_id=1, source_target_pairs={{0,16},{8,24},{16,32},{24,40},{32,48},{40,56},{48,64},{56,72},{64,... | collective-permute-start | bytes 98312
  562.4 6.0 %collective-permute-start.18 = (f32[64,128]{1,0:T(8,128)}, f32[64,128]{1,0:T(8,128)S(1)}, u32[]{:S(2)}, u32[]{:S(2)}) collective-permute-start(f32[64,128]{1,0:T(8,128)} %get-tuple-element.27), channel_id=1, source_target_pairs={{0,8},{8,16},{16,24},{24,32},{32,40},{40,48},{48,56},{56,64},{64,7... | collective-permute-start | bytes 98312
Sparse Core Ops, SparseCore 0:
  182.2 71.5 all-reduce.8
  256.2 48.4 all-gather.3
